TPU v7x, 32 devices: a whole 2x2x4 slice. The times are simulated.
32 devices in a mesh: segment: 4 (over y, x), dom: 8 (over z, core).
Axes of the slice: x: 2, y: 2, z: 4, core: 2. Of those that a mesh axis runs over, the one named last changes fastest.
Arguments:
- forward_held: float32 [4, 2048, 512], P('segment', 'dom'), may hold values from -6 to 6
- forward_new: float32 [2048, 512], P('dom'), may hold values from -6 to 6
- back_outputs: float32 [4, 2048, 512], P('segment', 'dom'), may hold values from -6 to 6
- back_cotangents: float32 [4, 2048, 512], P('segment', 'dom'), may hold values from -6 to 6
- back_new_outputs: float32 [2048, 512], P('dom'), may hold values from -6 to 6
- back_new_cotangents: float32 [2048, 512], P('dom'), may hold values from -6 to 6
- adj_tiles: float32 [16, 16, 128, 128], P('dom'), may hold values from 0 to 0.046875, as said below
- tile_cols: int32 [16, 16], P('dom'), may hold values from 0 to 15, as said below
- weight_first: float32 [8, 256, 256], P('segment'), may hold values from -0.375 to 0.375
- weight_second: float32 [8, 256, 256], P('segment'), may hold values from -0.375 to 0.375
- gain_first: float32 [8, 256], P('segment'), may hold values from 0.1 to 1.9
- gain_second: float32 [8, 256], P('segment'), may hold values from 0.1 to 1.9
Outputs:
- forward_one: float32 [4, 2048, 512], P('segment', 'dom')
- forward_two: float32 [4, 2048, 512], P('segment', 'dom')
- inputs_one: float32 [4, 2048, 512], P('segment', 'dom')
- cotan_one: float32 [4, 2048, 512], P('segment', 'dom')
- inputs_two: float32 [4, 2048, 512], P('segment', 'dom')
- cotan_two: float32 [4, 2048, 512], P('segment', 'dom')
- grad_weight_first: float32 [8, 256, 256], P('segment')
- grad_weight_second: float32 [8, 256, 256], P('segment')
- grad_gain_first: float32 [8, 256], P('segment')
- grad_gain_second: float32 [8, 256], P('segment')
Inputs may be any that keep to these rules, and one draw needn't show every extreme that they name: tile_cols[r, t] lies between max(0, (r // 2 - 1) * 2) and min(16, (r // 2 + 2) * 2) - 1: a block of the row block's own partition or of the partition on either side; a column block may appear several times in a row. `adj_tiles`: each entry is zero or positive; a node's row over its 16 tiles holds about 32 nonzero entries, and its expected sum is one.
All inputs are finite; a program needn't handle non-finite values.
Results may differ from a plain program's by a relative error of at most 0.00085.
Values sent between devices are 32-bit elements; how exact they have to be, the bound alone decides.
A program may use at most 128 MiB of HBM per device.

v0:
```python
import functools
import math

import jax
import jax.numpy as jnp
from jax import lax
from jax.experimental import pallas as pl
from jax.experimental.pallas import tpu as pltpu
from jax.sharding import PartitionSpec as P

MESH = pl.DeviceIdType.MESH
F32 = jnp.float32
BF16 = jnp.bfloat16


def split(value):
    high = value.astype(BF16)
    return high, (value - high.astype(F32)).astype(BF16)


def split6(value):
    high = value.astype(BF16)
    rest = value - high.astype(F32)
    mid = rest.astype(BF16)
    return high, mid, (rest - mid.astype(F32)).astype(BF16)


def dot(a, b, dims=((1,), (0,))):
    return lax.dot_general(a, b, (dims, ((), ())), preferred_element_type=F32)


def dot3(a, b, dims=((1,), (0,))):
    (ah, al), (bh, bl) = a, b
    return dot(ah, bh, dims) + (dot(ah, bl, dims) + dot(al, bh, dims))


def dot6(a, b):
    (ah, am, al), (bh, bm, bl) = a, b
    small = dot(ah, bl) + dot(al, bh) + dot(am, bm)
    return dot(ah, bh) + (dot(ah, bm) + dot(am, bh) + small)


def kernel(
    doms,
    segs,
    cols,
    fwd_in,
    fwd_new,
    out_in,
    cot_in,
    out_new,
    cot_new,
    tiles,
    wf,
    ws,
    gf,
    gs,
    fwd_one,
    fwd_two,
    in_one,
    ct_one,
    in_two,
    ct_two,
    gwf,
    gws,
    ggf,
    ggs,
    band_h,
    band_l,
    band_x,
    bt_h,
    bt_l,
    w_h,
    w_l,
    w_x,
    st,
    ext,
    ks,
    kr,
    km,
    xh,
    rs,
    hold,
    land,
    grad,
    gland,
    gout,
    send_sem,
    recv_sem,
    hs_sem,
    hr_sem,
    gs_sem,
    gr_sem,
):
    dom = lax.axis_index("dom")
    seg = lax.axis_index("segment")
    S = fwd_new.shape[0]
    H = fwd_new.shape[1] // 2
    L = wf.shape[0]
    rounds = 2 * L
    bits = doms.bit_length() - 1
    has_left, has_right = dom > 0, dom < doms - 1
    has_prev, has_next = seg > 0, seg < segs - 1

    def partner(s):
        bit = (dom // (1 << s)) % 2
        return bit, dom + (1 << s) * (1 - 2 * bit)

    barrier = pltpu.get_barrier_semaphore()

    def greet(where):
        pl.semaphore_signal(barrier, inc=1, device_id=where, device_id_type=MESH)

    for cond, where in (
        (has_left, {"dom": dom - 1}),
        (has_right, {"dom": dom + 1}),
        (has_prev, {"segment": seg - 1}),
        (has_next, {"segment": seg + 1}),
    ):
        pl.when(cond)(functools.partial(greet, where))
    for s in range(bits):
        greet({"dom": partner(s)[1]})

    R, T, B = tiles.shape[0], tiles.shape[1], tiles.shape[2]
    first = (dom - 1) * R
    for r in range(R):
        for w in range(3 * R):
            total = jnp.zeros((B, B), F32)
            for t in range(T):
                total += jnp.where(cols[r, t] == first + w, 1.0, 0.0) * tiles[r, t]
            hi, lo, rest = split6(total)
            band_x[r * B : (r + 1) * B, w * B : (w + 1) * B] = rest
            band_h[r * B : (r + 1) * B, w * B : (w + 1) * B] = hi
            band_l[r * B : (r + 1) * B, w * B : (w + 1) * B] = lo
            hi, lo = split(total.T)
            bt_h[w * B : (w + 1) * B, r * B : (r + 1) * B] = hi
            bt_l[w * B : (w + 1) * B, r * B : (r + 1) * B] = lo
    for j in range(L):
        for k, ref in enumerate((wf, ws)):
            w_h[2 * j + k], w_l[2 * j + k], w_x[2 * j + k] = split6(ref[j])
    grad[...] = jnp.zeros_like(grad)
    zero = jnp.zeros((S, H), F32)

    @pl.when(jnp.logical_not(has_left))
    def _():
        for par in range(2):
            ext[0, par, :S] = zero
            ext[1, par, :S] = zero
            kr[par, :S] = zero

    @pl.when(jnp.logical_not(has_right))
    def _():
        for par in range(2):
            ext[0, par, 2 * S :] = zero
            ext[1, par, 2 * S :] = zero
            kr[par, S:] = zero

    expected = (
        bits
        + has_left.astype(jnp.int32)
        + has_right.astype(jnp.int32)
        + has_prev.astype(jnp.int32)
        + has_next.astype(jnp.int32)
    )
    pl.semaphore_wait(barrier, expected)

    def to_left(chain, par):
        if chain == 2:
            src, dst = ks.at[par, :S], kr.at[par, S:]
        else:
            src, dst = ext.at[chain, par, S : 2 * S], ext.at[chain, par, 2 * S :]
        return pltpu.make_async_remote_copy(
            src, dst, send_sem.at[chain, par, 0], recv_sem.at[chain, par, 0],
            device_id={"dom": dom - 1}, device_id_type=MESH,
        )

    def to_right(chain, par):
        if chain == 2:
            src, dst = ks.at[par, S:], kr.at[par, :S]
        else:
            src, dst = ext.at[chain, par, S : 2 * S], ext.at[chain, par, :S]
        return pltpu.make_async_remote_copy(
            src, dst, send_sem.at[chain, par, 1], recv_sem.at[chain, par, 1],
            device_id={"dom": dom + 1}, device_id_type=MESH,
        )

    def start(chain, par):
        @pl.when(has_left)
        def _():
            to_left(chain, par).start()

        @pl.when(has_right)
        def _():
            to_right(chain, par).start()

    def finish(chain, par):
        @pl.when(has_left)
        def _():
            to_left(chain, par).wait_send()
            to_right(chain, par).wait_recv()

        @pl.when(has_right)
        def _():
            to_right(chain, par).wait_send()
            to_left(chain, par).wait_recv()

    def normed(value):
        centred = value - jnp.mean(value, axis=1, keepdims=True)
        scale = lax.rsqrt(jnp.mean(centred * centred, axis=1, keepdims=True) + 1e-05)
        return centred * scale, scale

    def weight(index):
        return w_h[index], w_l[index]

    def gain(index):
        return (gf, gs)[index % 2][index // 2 : index // 2 + 1, :]

    def emit_forward(r):
        par = r % 2
        xhat, _ = normed(st[1 - par])
        ext[0, par, S : 2 * S] = dot3(split(jnp.maximum(xhat * gain(r), 0.0)), weight(r))
        start(0, par)

    def emit_inverse(r):
        par, index = r % 2, rounds - 1 - r
        xhat, scale = normed(st[2 + par])
        xh[par] = xhat
        rs[par] = scale
        ext[1, par, S : 2 * S] = dot6(
            split6(jnp.maximum(xhat * gain(index), 0.0)), weight(index) + (w_x[index],)
        )
        start(1, par)

    def emit_cotan(r):
        par = r % 2
        value = split(st[5 - par])
        for place in range(2):
            lo, hi = 2 * place * S, (2 * place + 1) * S
            ks[par, place * S : (place + 1) * S] = dot3((bt_h[lo:hi], bt_l[lo:hi]), value)
        start(2, par)
        km[...] = dot3((bt_h[S : 2 * S], bt_l[S : 2 * S]), value)


    def end_forward(r):
        par = r % 2
        finish(0, par)
        st[par] += dot3((band_h[...], band_l[...]), split(ext[0, par]))

    def end_inverse(r):
        par = r % 2
        finish(1, par)
        st[3 - par] -= dot6((band_h[...], band_l[...], band_x[...]), split6(ext[1, par]))

    def end_cotan(r):
        par, index = r % 2, rounds - 1 - r
        finish(2, par)
        total = km[...] + (kr[par, :S] + kr[par, S:])
        parts = split(total)
        xhat = xh[par]
        vec = gain(index)
        pre = xhat * vec
        back = dot3(parts, weight(index), ((1,), (1,)))
        back = jnp.where(pre > 0.0, back, 0.0)
        row = rounds * H + index
        grad[row : row + 1, :] += jnp.sum(back * xhat, axis=0, keepdims=True)
        back = back * vec
        inner = jnp.mean(back * xhat, axis=1, keepdims=True)
        st[4 + par] += rs[par] * (back - jnp.mean(back, axis=1, keepdims=True) - xhat * inner)
        rows = jnp.maximum(pre, 0.0).T
        grad[index * H : (index + 1) * H, :] += dot3(split(rows), parts)

    outs = ((fwd_one, fwd_two), (in_one, in_two), (ct_one, ct_two))

    def hand(chain, half):
        ahead = 1 if chain == 0 else -1
        k = 2 * chain + half
        return pltpu.make_async_remote_copy(
            hold.at[k], land.at[k],
            hs_sem.at[k], hr_sem.at[k],
            device_id={"segment": seg + ahead}, device_id_type=MESH,
        )

    def can_send(chain):
        return has_next if chain == 0 else has_prev

    def can_take(chain):
        return has_prev if chain == 0 else has_next

    def store(slot, chain, half):
        @pl.when(slot == 0)
        def _():
            outs[chain][0][0, :, half * H : (half + 1) * H] = st[2 * chain + half]
            hold[2 * chain + half] = st[2 * chain + half]
            pl.when(can_send(chain))(lambda: hand(chain, half).start())

        @pl.when(slot == 1)
        def _():
            outs[chain][1][0, :, half * H : (half + 1) * H] = st[2 * chain + half]

    olds, news = (fwd_in, out_in, cot_in), (fwd_new, out_new, cot_new)

    def load(slot, chain):
        @pl.when(slot == 0)
        def _():
            for half in range(2):
                st[2 * chain + half] = olds[chain][0, :, half * H : (half + 1) * H]

        @pl.when(jnp.logical_and(slot == 1, jnp.logical_not(can_take(chain))))
        def _():
            for half in range(2):
                st[2 * chain + half] = news[chain][:, half * H : (half + 1) * H]

        @pl.when(jnp.logical_and(slot == 1, can_take(chain)))
        def _():
            for half in range(2):
                hand(chain, half).wait_recv()
                st[2 * chain + half] = land[2 * chain + half]

    emits = (emit_forward, emit_inverse, emit_cotan)
    ends = (end_forward, end_inverse, end_cotan)

    def run_slot(slot, carry):
        for chain in range(3):
            load(slot, chain)
            emits[chain](0)
        for r in range(rounds):
            for chain in range(3):
                ends[chain](r)
                if r + 1 < rounds:
                    emits[chain](r + 1)
                if r >= rounds - 2:
                    store(slot, chain, r % 2 if chain != 1 else 1 - r % 2)
        return carry

    lax.fori_loop(0, 2, run_slot, 0)

    rows = grad.shape[0]
    offset, size, used = 0, rows, 0
    steps = []
    for s in range(bits):
        bit, other = partner(s)
        size = size // 2
        keep = pl.multiple_of(offset + bit * size, 8)
        give = pl.multiple_of(offset + (1 - bit) * size, 8)
        copy = pltpu.make_async_remote_copy(
            grad.at[pl.ds(give, size)], gland.at[used : used + size],
            gs_sem.at[0, s], gr_sem.at[0, s],
            device_id={"dom": other}, device_id_type=MESH,
        )
        copy.start()
        copy.wait()
        grad[pl.ds(keep, size), :] += gland[used : used + size, :]
        steps.append((s, other, keep, size))
        used, offset = used + size, keep
    gout[pl.ds(offset, size), :] = grad[pl.ds(offset, size), :]
    for s, other, keep, size in reversed(steps):
        copy = pltpu.make_async_remote_copy(
            gout.at[pl.ds(keep, size)], gout.at[pl.ds(keep, size)],
            gs_sem.at[1, s], gr_sem.at[1, s],
            device_id={"dom": other}, device_id_type=MESH,
        )
        copy.start()
        copy.wait()
    scale = 1.0 / math.sqrt(2.0 * S * doms)
    for j in range(L):
        for k, (wref, gref) in enumerate(((gwf, ggf), (gws, ggs))):
            index = 2 * j + k
            wref[j] = gout[index * H : (index + 1) * H, :] * scale
            row = rounds * H + index
            gref[j : j + 1, :] = gout[row : row + 1, :] * scale
    for chain in range(3):
        for half in range(2):
            pl.when(can_send(chain))(lambda c=chain, h=half: hand(c, h).wait_send())


def per_device(doms, segs, *args):
    (held, new, bo, bc, bno, bnc, tiles, cols, wf, ws, gf, gs) = args
    S, W = new.shape
    H, L = W // 2, wf.shape[0]
    bits = doms.bit_length() - 1
    rows = 2 * L * H + 8 * doms
    state = jax.ShapeDtypeStruct((1, S, W), F32)
    vmem = pl.BlockSpec(memory_space=pltpu.VMEM)
    results = pl.pallas_call(
        functools.partial(kernel, doms, segs),
        out_shape=[state] * 6
        + [jax.ShapeDtypeStruct((L, H, H), F32)] * 2
        + [jax.ShapeDtypeStruct((L, H), F32)] * 2,
        in_specs=[pl.BlockSpec(memory_space=pltpu.SMEM)] + [vmem] * 11,
        out_specs=[vmem] * 10,
        scratch_shapes=[
            pltpu.VMEM((S, 3 * S), BF16),
            pltpu.VMEM((S, 3 * S), BF16),
            pltpu.VMEM((S, 3 * S), BF16),
            pltpu.VMEM((3 * S, S), BF16),
            pltpu.VMEM((3 * S, S), BF16),
            pltpu.VMEM((2 * L, H, H), BF16),
            pltpu.VMEM((2 * L, H, H), BF16),
            pltpu.VMEM((2 * L, H, H), BF16),
            pltpu.VMEM((6, S, H), F32),
            pltpu.VMEM((2, 2, 3 * S, H), F32),
            pltpu.VMEM((2, 2 * S, H), F32),
            pltpu.VMEM((2, 2 * S, H), F32),
            pltpu.VMEM((S, H), F32),
            pltpu.VMEM((2, S, H), F32),
            pltpu.VMEM((2, S, 1), F32),
            pltpu.VMEM((6, S, H), F32),
            pltpu.VMEM((6, S, H), F32),
            pltpu.VMEM((rows, H), F32),
            pltpu.VMEM((rows, H), F32),
            pltpu.VMEM((rows, H), F32),
            pltpu.SemaphoreType.DMA((3, 2, 2)),
            pltpu.SemaphoreType.DMA((3, 2, 2)),
            pltpu.SemaphoreType.DMA((6,)),
            pltpu.SemaphoreType.DMA((6,)),
            pltpu.SemaphoreType.DMA((2, bits)),
            pltpu.SemaphoreType.DMA((2, bits)),
        ],
        compiler_params=pltpu.CompilerParams(
            collective_id=0, has_side_effects=True, vmem_limit_bytes=60 * 1024 * 1024
        ),
    )(cols, held, new, bo, bc, bno, bnc, tiles, wf, ws, gf, gs)
    return tuple(results)


def solution(mesh):
    row = P("segment", "dom", None)
    flat = P("dom", None)
    cube = P("segment", None, None)
    vec = P("segment", None)
    return jax.shard_map(
        functools.partial(per_device, mesh.shape["dom"], mesh.shape["segment"]),
        mesh=mesh,
        in_specs=(
            row, flat, row, row, flat, flat,
            P("dom", None, None, None), flat, cube, cube, vec, vec,
        ),
        out_specs=(row,) * 6 + (cube, cube, vec, vec),
        check_vma=False,
    )
```

profile of v0, /device:TPU:0, one launch (start us, length us, event | category | flops | bytes accessed | tf_op | source)
XLA Modules:
  0.0 143.0 jit_solution(8327614935578014064)
XLA Ops:
  0.6 132.5 %shard_map.195 = (f32[1,256,512]{2,1,0:T(8,128)}, f32[1,256,512]{2,1,0:T(8,128)}, f32[1,256,512]{2,1,0:T(8,128)}, f32[1,256,512]{2,1,0:T(8,128)}, f32[1,256,512]...) custom-call(s32[2,16]{1,0:T(2,128)} %cols.1, ...), custom_call_target="tpu_custom_call" | custom-call | tf_op jit(solution)/shard_map/pallas_call | solution.py:384
  133.2 0.0 copy-start.5
  133.2 0.0 copy-start.4
  133.2 0.0 copy-start.3
  133.2 2.0 %copy.32 = f32[1,256,512]{2,1,0:T(8,128)} copy(f32[1,256,512]{2,1,0:T(8,128)} %get-tuple-element.20) | data formatting | bytes 1048576
  135.2 0.0 copy-start.2
  135.2 1.9 %copy.33 = f32[1,256,512]{2,1,0:T(8,128)} copy(f32[1,256,512]{2,1,0:T(8,128)} %get-tuple-element.21) | data formatting | bytes 1048576
  137.1 0.0 copy-done.5
  137.1 0.0 copy-start.1
  137.1 0.8 copy.34
  137.9 0.0 copy-done.4
  137.9 0.8 copy.35
  138.7 0.0 copy-done.3
  138.7 0.8 copy.36
  139.5 0.0 copy-done.2
  139.5 0.8 copy.37
  140.3 0.0 copy-done.1
  140.3 0.8 copy.38
  141.1 0.0 copy-done
  141.1 0.8 copy.39
  141.9 0.0 copy-done.7
  141.9 0.6 copy.40
  142.5 0.0 copy-done.6
  142.5 0.6 copy.41
  (3 shorter events, 0.0 us)
Async XLA Ops:
  133.2 3.9 %copy-start.5 = (f32[1,256,512]{2,1,0:T(8,128)S(1)}, f32[1,256,512]{2,1,0:T(8,128)}, u32[]{:S(2)}) copy-start(f32[1,256,512]{2,1,0:T(8,128)} %get-tuple-element.22) | copy-start | bytes 1572868
  133.2 4.7 %copy-start.4 = (f32[1,256,512]{2,1,0:T(8,128)S(1)}, f32[1,256,512]{2,1,0:T(8,128)}, u32[]{:S(2)}) copy-start(f32[1,256,512]{2,1,0:T(8,128)} %get-tuple-element.23) | copy-start | bytes 1572868
  133.2 5.5 %copy-start.3 = (f32[1,256,512]{2,1,0:T(8,128)S(1)}, f32[1,256,512]{2,1,0:T(8,128)}, u32[]{:S(2)}) copy-start(f32[1,256,512]{2,1,0:T(8,128)} %get-tuple-element.24) | copy-start | bytes 1572868
  135.2 4.3 %copy-start.2 = (f32[1,256,512]{2,1,0:T(8,128)S(1)}, f32[1,256,512]{2,1,0:T(8,128)}, u32[]{:S(2)}) copy-start(f32[1,256,512]{2,1,0:T(8,128)} %get-tuple-element.25) | copy-start | bytes 1572868
  137.1 3.2 %copy-start.1 = (f32[2,256,256]{2,1,0:T(8,128)S(1)}, f32[2,256,256]{2,1,0:T(8,128)}, u32[]{:S(2)}) copy-start(f32[2,256,256]{2,1,0:T(8,128)} %get-tuple-element.26) | copy-start | bytes 1572868
  137.9 3.2 %copy-start = (f32[2,256,256]{2,1,0:T(8,128)S(1)}, f32[2,256,256]{2,1,0:T(8,128)}, u32[]{:S(2)}) copy-start(f32[2,256,256]{2,1,0:T(8,128)} %get-tuple-element.27) | copy-start | bytes 1572868
  138.7 3.2 %copy-start.7 = (f32[2,256]{1,0:T(2,128)S(1)}, f32[2,256]{1,0:T(2,128)}, u32[]{:S(2)}) copy-start(f32[2,256]{1,0:T(2,128)} %get-tuple-element.28) | copy-start | bytes 6148
  138.7 3.8 %copy-start.6 = (f32[2,256]{1,0:T(2,128)S(1)}, f32[2,256]{1,0:T(2,128)}, u32[]{:S(2)}) copy-start(f32[2,256]{1,0:T(2,128)} %get-tuple-element.29) | copy-start | bytes 6148
where the time goes:
time: 143 us
  Pallas kernels  132 us (92%)
  local copies, waits for them, and re-layouts  9.85 us (7%)
    pallas_call x1, Pallas kernels, per_device(): pl.pallas_call(functools.partial(kernel, doms, segs), out_shape=[state] *...  132 us
    unnamed x26, local copies, waits for them, and re-layouts  9.85 us

commit v1 on v0

--- a/solution.py
+++ b/solution.py
@@ -267,7 +267,8 @@
         inner = jnp.mean(back * xhat, axis=1, keepdims=True)
         st[4 + par] += rs[par] * (back - jnp.mean(back, axis=1, keepdims=True) - xhat * inner)
         rows = jnp.maximum(pre, 0.0).T
-        grad[index * H : (index + 1) * H, :] += dot3(split(rows), parts)
+        base = (rounds - 1 - index) * H
+        grad[base : base + H, :] += dot3(split(rows), parts)
 
     outs = ((fwd_one, fwd_two), (in_one, in_two), (ct_one, ct_two))
 
@@ -316,10 +317,54 @@
                 hand(chain, half).wait_recv()
                 st[2 * chain + half] = land[2 * chain + half]
 
+    plans, landed = [], 0
+    for q in range(rounds):
+        offset, size = q * H, H if q + 1 < rounds else grad.shape[0] - q * H
+        halvings, doublings = [], []
+        for s in range(bits):
+            bit, other = partner(s)
+            give = offset
+            if size % 16 == 0:
+                size = size // 2
+                give = pl.multiple_of(offset + (1 - bit) * size, 8)
+                offset = pl.multiple_of(offset + bit * size, 8)
+                doublings.insert(0, (other, offset, offset, size, None))
+            halvings.append((other, give, offset, size, landed))
+            landed += size
+        plans.append(halvings + doublings)
+    pointer = [0] * rounds
+
+    def piece(q, phase):
+        other, give, keep, size, place = plans[q][phase]
+        if place is None:
+            src, dst = gout.at[pl.ds(give, size)], gout.at[pl.ds(give, size)]
+        else:
+            src, dst = grad.at[pl.ds(give, size)], gland.at[place : place + size]
+        return pltpu.make_async_remote_copy(
+            src, dst, gs_sem.at[q, phase], gr_sem.at[q, phase],
+            device_id={"dom": other}, device_id_type=MESH,
+        )
+
+    def pump(q):
+        phase = pointer[q]
+        pointer[q] = phase + 1
+        if 0 < phase <= len(plans[q]):
+            piece(q, phase - 1).wait()
+            other, give, keep, size, place = plans[q][phase - 1]
+            if place is not None:
+                total = grad[pl.ds(keep, size), :] + gland[place : place + size, :]
+                if phase == bits:
+                    gout[pl.ds(keep, size), :] = total
+                else:
+                    grad[pl.ds(keep, size), :] = total
+        if phase < len(plans[q]):
+            piece(q, phase).start()
+
     emits = (emit_forward, emit_inverse, emit_cotan)
     ends = (end_forward, end_inverse, end_cotan)
 
     def run_slot(slot, carry):
+        pointer[:] = [0] * rounds
         for chain in range(3):
             load(slot, chain)
             emits[chain](0)
@@ -328,49 +373,47 @@
                 ends[chain](r)
                 if r + 1 < rounds:
                     emits[chain](r + 1)
+                ready = range(r + 1 if chain == 2 else r)
+                if ready:
+
+                    @pl.when(slot == 1)
+                    def _():
+                        for q in ready:
+                            if q + 1 < rounds:
+                                pump(q)
+
                 if r >= rounds - 2:
                     store(slot, chain, r % 2 if chain != 1 else 1 - r % 2)
         return carry
 
     lax.fori_loop(0, 2, run_slot, 0)
 
-    rows = grad.shape[0]
-    offset, size, used = 0, rows, 0
-    steps = []
-    for s in range(bits):
-        bit, other = partner(s)
-        size = size // 2
-        keep = pl.multiple_of(offset + bit * size, 8)
-        give = pl.multiple_of(offset + (1 - bit) * size, 8)
-        copy = pltpu.make_async_remote_copy(
-            grad.at[pl.ds(give, size)], gland.at[used : used + size],
-            gs_sem.at[0, s], gr_sem.at[0, s],
-            device_id={"dom": other}, device_id_type=MESH,
-        )
-        copy.start()
-        copy.wait()
-        grad[pl.ds(keep, size), :] += gland[used : used + size, :]
-        steps.append((s, other, keep, size))
-        used, offset = used + size, keep
-    gout[pl.ds(offset, size), :] = grad[pl.ds(offset, size), :]
-    for s, other, keep, size in reversed(steps):
-        copy = pltpu.make_async_remote_copy(
-            gout.at[pl.ds(keep, size)], gout.at[pl.ds(keep, size)],
-            gs_sem.at[1, s], gr_sem.at[1, s],
-            device_id={"dom": other}, device_id_type=MESH,
-        )
-        copy.start()
-        copy.wait()
+    while any(pointer[q] <= len(plans[q]) for q in range(rounds)):
+        for q in range(rounds):
+            pump(q)
     scale = 1.0 / math.sqrt(2.0 * S * doms)
     for j in range(L):
         for k, (wref, gref) in enumerate(((gwf, ggf), (gws, ggs))):
             index = 2 * j + k
-            wref[j] = gout[index * H : (index + 1) * H, :] * scale
+            base = (rounds - 1 - index) * H
+            wref[j] = gout[base : base + H, :] * scale
             row = rounds * H + index
             gref[j : j + 1, :] = gout[row : row + 1, :] * scale
     for chain in range(3):
         for half in range(2):
             pl.when(can_send(chain))(lambda c=chain, h=half: hand(c, h).wait_send())
+
+
+def publish(*refs):
+    sems = refs[-1]
+    count = len(refs) // 2
+    copies = [
+        pltpu.make_async_copy(refs[i], refs[count + i], sems.at[i]) for i in range(count)
+    ]
+    for copy in copies:
+        copy.start()
+    for copy in copies:
+        copy.wait()
 
 
 def per_device(doms, segs, *args):
@@ -407,20 +450,30 @@
             pltpu.VMEM((6, S, H), F32),
             pltpu.VMEM((6, S, H), F32),
             pltpu.VMEM((rows, H), F32),
-            pltpu.VMEM((rows, H), F32),
+            pltpu.VMEM((2 * rows, H), F32),
             pltpu.VMEM((rows, H), F32),
             pltpu.SemaphoreType.DMA((3, 2, 2)),
             pltpu.SemaphoreType.DMA((3, 2, 2)),
             pltpu.SemaphoreType.DMA((6,)),
             pltpu.SemaphoreType.DMA((6,)),
-            pltpu.SemaphoreType.DMA((2, bits)),
-            pltpu.SemaphoreType.DMA((2, bits)),
+            pltpu.SemaphoreType.DMA((2 * L, 2 * bits)),
+            pltpu.SemaphoreType.DMA((2 * L, 2 * bits)),
         ],
         compiler_params=pltpu.CompilerParams(
             collective_id=0, has_side_effects=True, vmem_limit_bytes=60 * 1024 * 1024
         ),
     )(cols, held, new, bo, bc, bno, bnc, tiles, wf, ws, gf, gs)
-    return tuple(results)
+    shapes = [jax.ShapeDtypeStruct(r.shape, r.dtype) for r in results]
+    count = len(shapes)
+    return tuple(
+        pl.pallas_call(
+            publish,
+            out_shape=shapes,
+            in_specs=[vmem] * count,
+            out_specs=[pl.BlockSpec(memory_space=pl.ANY)] * count,
+            scratch_shapes=[pltpu.SemaphoreType.DMA((count,))],
+        )(*results)
+    )
 
 
 def solution(mesh):

time: 143 us -> 144 us (level)
  Pallas kernels: 132 us -> 143 us
  local copies, waits for them, and re-layouts: 9.85 us -> 0 us
    unnamed x26 -> x0, local copies, waits for them, and re-layouts: 9.85 us -> none
    pallas_call x1, Pallas kernels: 132 us -> 139 us  [per_device(): pl.pallas_call(functools.partial(kernel, doms, segs), out_shape=[state] *...]
    pallas_call x0 -> x1, Pallas kernels: none -> 4.25 us  [per_device(): pl.pallas_call(publish, out_shape=shapes, in_specs=[vmem] * count, out_sp...]
where the time goes in v1:
time: 144 us
  Pallas kernels  143 us (99%)
    pallas_call x1, Pallas kernels, per_device(): pl.pallas_call(functools.partial(kernel, doms, segs), out_shape=[state] *...  139 us
    pallas_call x1, Pallas kernels, per_device(): pl.pallas_call(publish, out_shape=shapes, in_specs=[vmem] * count, out_sp...  4.25 us

profile of v1, /device:TPU:0, one launch (start us, length us, event | category | flops | bytes accessed | tf_op | source)
XLA Modules:
  0.0 143.7 jit_solution(17567922814002210080)
XLA Ops:
  0.6 138.8 %shard_map.195 = (f32[1,256,512]{2,1,0:T(8,128)}, f32[1,256,512]{2,1,0:T(8,128)}, f32[1,256,512]{2,1,0:T(8,128)}, f32[1,256,512]{2,1,0:T(8,128)}, f32[1,256,512]...) custom-call(s32[2,16]{1,0:T(2,128)} %cols.1, ...), custom_call_target="tpu_custom_call" | custom-call | tf_op jit(solution)/shard_map/pallas_call | solution.py:427
  139.5 4.3 %shard_map.196 = (f32[1,256,512]{2,1,0:T(8,128)}, f32[1,256,512]{2,1,0:T(8,128)}, f32[1,256,512]{2,1,0:T(8,128)}, f32[1,256,512]{2,1,0:T(8,128)}, f32[1,256,512]...) custom-call(f32[1,256,512]{2,1,0:T(8,128)} %get-tuple-element.20.ref, ...), custom_call_target="tpu_custom_call" | custom-call | tf_op jit(solution)/shard_map/pallas_call | solution.py:469

commit v2 on v1

--- a/solution.py
+++ b/solution.py
@@ -373,7 +373,7 @@
                 ends[chain](r)
                 if r + 1 < rounds:
                     emits[chain](r + 1)
-                ready = range(r + 1 if chain == 2 else r)
+                ready = range(r + 1) if chain == 2 else ()
                 if ready:
 
                     @pl.when(slot == 1)

time: 144 us -> 136 us (0.944)
  Pallas kernels: 143 us -> 135 us
    pallas_call x1, Pallas kernels: 139 us -> 131 us  [per_device(): pl.pallas_call(functools.partial(kernel, doms, segs), out_shape=[state] *...]
where the time goes in v2:
time: 136 us; the launch traced here: 135 us
  Pallas kernels  135 us (99%)
    pallas_call x1, Pallas kernels, per_device(): pl.pallas_call(functools.partial(kernel, doms, segs), out_shape=[state] *...  131 us
    pallas_call x1, Pallas kernels, per_device(): pl.pallas_call(publish, out_shape=shapes, in_specs=[vmem] * count, out_sp...  4.25 us

profile of v2, /device:TPU:0, one launch (start us, length us, event | category | flops | bytes accessed | tf_op | source)
XLA Modules:
  0.0 135.4 jit_solution(11639999601137441576)
XLA Ops:
  0.6 130.5 %shard_map.195 = (f32[1,256,512]{2,1,0:T(8,128)}, f32[1,256,512]{2,1,0:T(8,128)}, f32[1,256,512]{2,1,0:T(8,128)}, f32[1,256,512]{2,1,0:T(8,128)}, f32[1,256,512]...) custom-call(s32[2,16]{1,0:T(2,128)} %cols.1, ...), custom_call_target="tpu_custom_call" | custom-call | tf_op jit(solution)/shard_map/pallas_call | solution.py:427
  131.2 4.3 %shard_map.196 = (f32[1,256,512]{2,1,0:T(8,128)}, f32[1,256,512]{2,1,0:T(8,128)}, f32[1,256,512]{2,1,0:T(8,128)}, f32[1,256,512]{2,1,0:T(8,128)}, f32[1,256,512]...) custom-call(f32[1,256,512]{2,1,0:T(8,128)} %get-tuple-element.20.ref, ...), custom_call_target="tpu_custom_call" | custom-call | tf_op jit(solution)/shard_map/pallas_call | solution.py:469
